TPU v7x, 256 devices: a whole 4x4x8 slice. The times are simulated.
256 devices in a mesh: seq: 64 (over y, z, core), head: 4 (over x).
Axes of the slice: x: 4, y: 4, z: 8, core: 2. Of those that a mesh axis runs over, the one named last changes fastest.
Arguments:
- queries: bfloat16 [12288, 4096], P('seq', 'head'), may hold values from -125 to 125
- key_vectors: bfloat16 [12288, 4096], P('seq', 'head'), may hold values from -21 to 21
- values: bfloat16 [12288, 4096], P('seq', 'head'), may hold values from -6 to 6
- cotangent: bfloat16 [12288, 4096], P('seq', 'head'), may hold values from -6 to 6
- cluster: int32 [12288, 1], P('seq'), may hold values from 0 to 15; in each aligned block of 192 rows (0 to 191, 192 to 383, ...) at most 24 rows name the same one
- block_pattern: int32 [16, 96, 96], replicated, may hold values from 0 to 1, as said below
Outputs:
- attended: bfloat16 [12288, 4096], P('seq', 'head')
- query_grad: bfloat16 [12288, 4096], P('seq', 'head')
- key_grad: bfloat16 [12288, 4096], P('seq', 'head')
- value_grad: bfloat16 [12288, 4096], P('seq', 'head')
Inputs may be any that keep to these rules, and one draw needn't show every extreme that they name: Within the rows of one device no cluster is named by more than 24 rows, and in every draw some cluster is named by exactly 24 rows of some device. Every diagonal entry block_pattern[g, b, b] is 1.
All inputs are finite; a program needn't handle non-finite values.
Results may differ from a plain program's by a relative error of at most 0.0061.
Values may be sent and summed in bfloat16 or wider, within the bound.
A program may use at most 128 MiB of HBM per device.

v0:
```python
import jax
import jax.numpy as jnp
from jax import lax
from jax.sharding import PartitionSpec as P

HEADS = 32
HEAD_DIM = 128
GS = 4
BLK = 128
NEG_FILL = -1e30
EPSILON = 1e-05


def from_partner(value, axis, bit):
    mask = 2**bit
    pairs = [(source, source ^ mask) for source in range(lax.axis_size(axis))]
    return lax.ppermute(value, axis, pairs)


def contract_last(left_side, right_side):
    return lax.dot_general(
        left_side, right_side, (((1,), (1,)), ((), ())), preferred_element_type=jnp.float32
    )


def contract_first(left_side, right_side):
    return lax.dot_general(
        left_side, right_side, (((0,), (0,)), ((), ())), preferred_element_type=jnp.float32
    )


def visible_mask(pattern, query_pos, query_live, key_pos, key_live):
    pattern_rows = pattern[query_pos // BLK]
    allowed = jnp.take(pattern_rows, key_pos // BLK, axis=1) == 1
    causal = key_pos[None, :] <= query_pos[:, None]
    return allowed & causal & query_live[:, None] & key_live[None, :]


def cluster_ranks(table, cluster_index):
    source_count, tok_count = table.shape
    in_cluster = table == cluster_index
    token_iota = jnp.arange(tok_count, dtype=jnp.int32)
    earlier_table = (token_iota[:, None] < token_iota[None, :]).astype(jnp.bfloat16)
    earlier = jnp.dot(
        in_cluster.astype(jnp.bfloat16), earlier_table, preferred_element_type=jnp.float32
    ).astype(jnp.int32)
    global_pos = (
        jnp.arange(source_count, dtype=jnp.int32)[:, None] * tok_count + token_iota[None, :]
    )
    return (in_cluster, earlier, global_pos)


def code_positions(slot_code, global_pos, capacity):
    matches = slot_code[:, :, None] == jnp.arange(capacity, dtype=jnp.int32)[None, None, :]
    positions = jnp.sum(jnp.where(matches, global_pos[:, :, None], 0), axis=1)
    occupied = jnp.any(matches, axis=1)
    return (positions, occupied)


def slot_positions(table, cluster_index, slot_count):
    source_count = table.shape[0]
    capacity = GS * slot_count
    in_cluster, earlier, global_pos = cluster_ranks(table, cluster_index)
    slot_code = jnp.where(in_cluster, earlier % GS * slot_count + earlier // GS, -1)
    positions, occupied = code_positions(slot_code, global_pos, capacity)
    positions = (
        positions.reshape(source_count, GS, slot_count)
        .transpose(1, 0, 2)
        .reshape(GS, source_count * slot_count)
    )
    occupied = (
        occupied.reshape(source_count, GS, slot_count)
        .transpose(1, 0, 2)
        .reshape(GS, source_count * slot_count)
    )
    return (positions, occupied)


def swap_keys(piece_now, bit_index):
    return from_partner(piece_now, "seq", bit_index)


def swap_grads(piece_now, bit_index):
    return from_partner(piece_now, "seq", bit_index)


def dispatch_rows(outgoing):
    return lax.all_to_all(outgoing, "seq", split_axis=1, concat_axis=1, tiled=True)


def combine_rows(outgoing):
    return lax.all_to_all(outgoing, "seq", split_axis=1, concat_axis=1, tiled=True)


def collect(local_piece, member, along, swapper):
    combined = local_piece
    for bit_index in range(GS.bit_length() - 1):
        partner_piece = swapper(combined, bit_index)
        lower_side = member // 2**bit_index % 2 == 0
        combined = jnp.where(
            lower_side,
            jnp.concatenate([combined, partner_piece], along),
            jnp.concatenate([partner_piece, combined], along),
        )
    return combined


def reduce_to_member(all_terms, member, swapper):
    current = all_terms
    for bit_index in reversed(range(GS.bit_length() - 1)):
        half_rows = current.shape[1] // 2
        lower_side = member // 2**bit_index % 2 == 0
        low_half = current[:, :half_rows]
        high_half = current[:, half_rows:]
        kept = jnp.where(lower_side, low_half, high_half)
        given = jnp.where(lower_side, high_half, low_half)
        current = kept + swapper(given, bit_index)
    return current


def forward_heads(query_slots, key_slots, value_slots, grad_slots, visible, score_scale):
    query_count, features = query_slots.shape
    key_count = key_slots.shape[0]
    head_count = features // HEAD_DIM
    attended = jnp.zeros((query_count, features), jnp.bfloat16)
    query_grad = jnp.zeros((query_count, features), jnp.bfloat16)
    side_result = jnp.zeros((2, key_count, features), jnp.float32)

    def one_head(head_index, running):
        attended_acc, query_acc, side_acc = running
        column_start = head_index * HEAD_DIM
        query_rows = lax.dynamic_slice_in_dim(query_slots, column_start, HEAD_DIM, 1)
        key_rows = lax.dynamic_slice_in_dim(key_slots, column_start, HEAD_DIM, 1)
        value_rows = lax.dynamic_slice_in_dim(value_slots, column_start, HEAD_DIM, 1)
        grad_rows = lax.dynamic_slice_in_dim(grad_slots, column_start, HEAD_DIM, 1)
        scores = jnp.where(visible, contract_last(query_rows, key_rows) * score_scale, NEG_FILL)
        row_max = jnp.max(scores, axis=1, keepdims=True)
        weights = jnp.where(visible, jnp.exp(scores - row_max), 0.0)
        row_total = jnp.maximum(jnp.sum(weights, axis=1, keepdims=True), 1.0)
        probabilities = weights / row_total
        prob_half = probabilities.astype(jnp.bfloat16)
        attended_head = jnp.dot(prob_half, value_rows, preferred_element_type=jnp.float32).astype(
            jnp.bfloat16
        )
        prob_grad = contract_last(grad_rows, value_rows)
        row_delta = jnp.sum(probabilities * prob_grad, axis=1, keepdims=True)
        score_grad = (probabilities * (prob_grad - row_delta)).astype(jnp.bfloat16)
        query_head = (
            jnp.dot(score_grad, key_rows, preferred_element_type=jnp.float32) * score_scale
        ).astype(jnp.bfloat16)
        attended_acc = lax.dynamic_update_slice_in_dim(attended_acc, attended_head, column_start, 1)
        query_acc = lax.dynamic_update_slice_in_dim(query_acc, query_head, column_start, 1)
        key_part = contract_first(score_grad, query_rows)
        value_part = contract_first(prob_half, grad_rows)
        side_acc = lax.dynamic_update_slice_in_dim(
            side_acc, jnp.stack([key_part, value_part]), column_start, 2
        )
        return (attended_acc, query_acc, side_acc)

    return lax.fori_loop(0, head_count, one_head, (attended, query_grad, side_result))


def per_device(queries, key_vectors, values, cotangent, cluster, block_pattern):
    seq_count = lax.axis_size("seq")
    tok_count, features = queries.shape
    slot_count = 2 * tok_count // seq_count
    received = seq_count * slot_count
    group_count = seq_count // GS
    score_scale = HEAD_DIM ** (-0.5)
    my_index = lax.axis_index("seq")
    group_index = my_index // GS
    member = my_index % GS
    key_float = key_vectors.astype(jnp.float32)
    square_sum = lax.psum(jnp.sum(key_float * key_float, axis=1), "head")
    key_rms = jnp.sqrt(square_sum / (HEADS * HEAD_DIM) + EPSILON)[:, None]
    normed_float = key_float / key_rms
    normed = normed_float.astype(jnp.bfloat16)
    own_ids = cluster[:, 0]
    everyone = lax.all_gather(own_ids, "seq", axis=0, tiled=True)
    table = everyone.reshape(seq_count, tok_count)
    token_iota = jnp.arange(tok_count, dtype=jnp.int32)
    onehot_own = (own_ids[:, None] == jnp.arange(group_count, dtype=jnp.int32)[None, :]).astype(
        jnp.bfloat16
    )
    before_table = (token_iota[:, None] > token_iota[None, :]).astype(jnp.bfloat16)
    before = jnp.dot(before_table, onehot_own, preferred_element_type=jnp.float32)
    own_rank = jnp.sum(before * onehot_own.astype(jnp.float32), axis=1).astype(jnp.int32)
    pattern = lax.dynamic_index_in_dim(block_pattern, group_index, 0, keepdims=False)
    stacked_inputs = jnp.stack([queries, normed, values, cotangent])
    destination = own_ids * GS + own_rank % GS
    send_slot = destination * slot_count + own_rank // GS
    outgoing = jnp.zeros((4, received, features), jnp.bfloat16).at[:, send_slot].set(stacked_inputs)
    arrived = dispatch_rows(outgoing)
    key_positions, key_present = slot_positions(table, group_index, slot_count)
    query_positions = lax.dynamic_index_in_dim(key_positions, member, 0, keepdims=False)
    query_present = lax.dynamic_index_in_dim(key_present, member, 0, keepdims=False)
    flat_positions = key_positions.reshape(-1)
    flat_present = key_present.reshape(-1)
    visible = visible_mask(pattern, query_positions, query_present, flat_positions, flat_present)
    key_value = collect(arrived[1:3], member, 1, swap_keys)
    attended, query_grad, both_terms = forward_heads(
        arrived[0], key_value[0], key_value[1], arrived[3], visible, score_scale
    )
    reduced = reduce_to_member(both_terms, member, swap_grads)
    key_part = reduced[0]
    value_part = reduced[1]
    normed_grad = (key_part * score_scale).astype(jnp.bfloat16)
    value_slots = value_part.astype(jnp.bfloat16)
    outgoing_back = jnp.stack([attended, query_grad, normed_grad, value_slots])
    returned = combine_rows(outgoing_back)
    home_rows = returned[:, send_slot]
    grad_float = home_rows[2].astype(jnp.float32)
    inner = lax.psum(jnp.sum(normed_float * grad_float, axis=1), "head")
    key_grad = (
        (grad_float - normed_float * (inner / (HEADS * HEAD_DIM))[:, None]) / key_rms
    ).astype(jnp.bfloat16)
    return (home_rows[0], home_rows[1], key_grad, home_rows[3])


def solution(mesh):
    in_specs = (
        P("seq", "head"),
        P("seq", "head"),
        P("seq", "head"),
        P("seq", "head"),
        P("seq", None),
        P(),
    )
    out_specs = (P("seq", "head"), P("seq", "head"), P("seq", "head"), P("seq", "head"))
    return jax.shard_map(
        per_device, mesh=mesh, in_specs=in_specs, out_specs=out_specs, check_vma=False
    )
```

profile of v0, /device:TPU:2, one launch (start us, length us, event | category | flops | bytes accessed | tf_op | source)
XLA Modules:
  0.0 935.9 jit_solution(13777769954462944271)
XLA Ops:
  3.5 10.0 %psum.14 = f32[192]{0:T(256)S(1)} all-reduce(f32[192]{0:T(256)S(1)} %fusion.30), channel_id=1, replica_groups=mesh['seq'=64,'head'=4] {'head'}, use_global_device_ids=true, to_apply=%region_2.3 | all-reduce | flops 192 | bytes 1536 | tf_op jit(solution)/shard_map/psum | solution.py:174
  17.2 2.5 broadcast_in_dim.72
  19.7 22.8 %scatter_fusion = bf16[4,384,1024]{2,0,1:T(4,128)(2,1)} fusion(bf16[4,384,1024]{2,0,1:T(4,128)(2,1)} %broadcast_in_dim.72, s32[192]{0:T(256)S(1)} %bitcast.92, bf16[192,4,1024]{2,1,0:T(4,128)(2,1)S(1)} %copy.35), kind=kCustom, calls=%fused_computation.3 | custom fusion | bytes 4719360 | tf_op jit(solution)/shard_map/scatter | solution.py:192
  42.5 83.7 %all_to_all.10 = bf16[4,384,1024]{2,0,1:T(4,128)(2,1)S(1)} all-to-all(bf16[4,384,1024]{2,0,1:T(4,128)(2,1)} %scatter_fusion), channel_id=1, replica_groups=mesh['seq'=64,'head'=4] {'seq'}, dimensions={1} | all-to-all | bytes 6291456 | tf_op jit(solution)/shard_map/all_to_all | solution.py:88
  126.2 1.7 copy-done.2
  127.9 1.8 slice.68
  131.8 248.5 %all-reduce = s32[12288]{0:T(1024)S(1)} all-reduce(s32[12288]{0:T(1024)S(1)} %dynamic-update-slice), channel_id=2, replica_groups=mesh['seq'=64,'head'=4] {'seq'}, use_global_device_ids=true, to_apply=%add | all-reduce | flops 12288 | bytes 98304
  380.4 16.6 %broadcast_select_fusion.2 = bf16[2,768,1024]{2,0,1:T(2,128)(2,1)} fusion(pred[]{:T(512)S(6)} %eq.66, bf16[2,384,1024]{2,0,1:T(2,128)(2,1)} %collective-permute-done, bf16[2,384,1024]{2,0,1:T(2,128)(2,1)S(1)} %slice.68), kind=kLoop, calls=%fused_computation.41 | loop fusion | flops 4718592 | bytes 6291457 | tf_op jit(solution)/shard_map/jit(_where)/select_n | solution.py:100
  402.7 3.7 gather_fusion.1
  408.7 2.2 fusion.52
  412.4 49.9 %collective-permute-done.1 = bf16[2,768,1024]{2,0,1:T(2,128)(2,1)} collective-permute-done((bf16[2,768,1024]{2,0,1:T(2,128)(2,1)}, bf16[2,768,1024]{2,0,1:T(2,128)(2,1)}, u32[]{:S(2)}, u32[]{:S(2)}) %collective-permute-start.1) | collective-permute-done | bytes 3145760 | tf_op jit(solution)/shard_map/ppermute | solution.py:17
  462.4 30.7 %broadcast_select_fusion = bf16[2,1536,1024]{2,0,1:T(2,128)(2,1)S(1)} fusion(pred[]{:T(512)S(6)} %eq.65, bf16[2,768,1024]{2,0,1:T(2,128)(2,1)} %collective-permute-done.1, bf16[2,768,1024]{2,0,1:T(2,128)(2,1)} %broadcast_select_fusion.2), kind=kLoop, calls=%fused_computation.38 | loop fusion | flops 9437184 | bytes 12582913 | tf_op jit(solution)/shard_map/jit(_where)/select_n | solution.py:100
  493.1 9.8 %fusion.51 = (bf16[1,1536,1024]{2,0,1:T(2,128)(2,1)S(1)}, bf16[1,1536,1024]{2,0,1:T(2,128)(2,1)}) fusion(bf16[2,1536,1024]{2,0,1:T(2,128)(2,1)S(1)} %broadcast_select_fusion), kind=kLoop, calls=%fused_computation.137 | loop fusion | bytes 12582912 | tf_op jit(solution)/shard_map/slice | solution.py:202
  502.9 8.0 copy_bitcast_fusion
  511.1 4.9 broadcast_in_dim.71.clone
  516.0 143.0 %while.17 = (s32[]{:T(128)}, bf16[384,1024]{1,0:T(8,128)(2,1)S(1)}, bf16[384,1024]{1,0:T(8,128)(2,1)S(1)}, f32[2,1536,1024]{2,0,1:T(2,128)}, bf16[384,1024]{1,0:...) while((s32[]{:T(128)}, bf16[384,1024]{1,0:T(8,128)(2,1)S(1)}, ...), condition=%wide.region_10.11_spmd, body=%wide.region_6.10_spmd.sunk | while | flops 915946752 | bytes 36587200 | solution.py:160
  527.4 1.7 fusion.77
  529.8 2.0 multiply_reduce_fusion.2
  537.2 6.7 copy_dynamic-update-slice_fusion.2
  546.2 2.0 multiply_reduce_fusion.2
  553.6 6.7 copy_dynamic-update-slice_fusion.2
  562.7 2.0 multiply_reduce_fusion.2
  570.1 6.7 copy_dynamic-update-slice_fusion.2
  579.2 2.0 multiply_reduce_fusion.2
  586.6 6.7 copy_dynamic-update-slice_fusion.2
  593.3 1.7 fusion.77
  595.7 2.0 multiply_reduce_fusion.2
  603.1 6.7 copy_dynamic-update-slice_fusion.2
  609.7 1.7 fusion.77
  612.1 2.0 multiply_reduce_fusion.2
  619.5 6.7 copy_dynamic-update-slice_fusion.2
  626.1 1.7 fusion.77
  628.5 2.0 multiply_reduce_fusion.2
  635.9 6.7 copy_dynamic-update-slice_fusion.2
  642.6 1.7 fusion.77
  645.0 2.0 multiply_reduce_fusion.2
  652.4 6.7 copy_dynamic-update-slice_fusion.2
  659.0 10.5 %broadcast_select_fusion.1 = f32[2,768,1024]{2,0,1:T(2,128)} fusion(pred[]{:T(512)S(6)} %eq.65, f32[2,1536,1024]{2,0,1:T(2,128)} %get-tuple-element.162), kind=kLoop, calls=%fused_computation.40 | loop fusion | flops 1572864 | bytes 18874368 | tf_op jit(solution)/shard_map/jit(_where)/select_n | solution.py:116
  669.7 131.3 %collective-permute-done.2 = f32[2,768,1024]{2,0,1:T(2,128)S(1)} collective-permute-done((f32[2,768,1024]{2,0,1:T(2,128)}, f32[2,768,1024]{2,0,1:T(2,128)S(1)}, u32[]{:S(2)}, u32[]{:S(2)}) %collective-permute-start.2) | collective-permute-done | bytes 6291488 | tf_op jit(solution)/shard_map/ppermute | solution.py:17
  801.1 10.0 %select_add_fusion = f32[2,768,1024]{2,0,1:T(2,128)S(1)} fusion(f32[2,768,1024]{2,0,1:T(2,128)S(1)} %collective-permute-done.2, pred[]{:T(512)S(6)} %eq.65, f32[2,1536,1024]{2,0,1:T(2,128)} %get-tuple-element.162), kind=kLoop, calls=%fused_computation.39 | loop fusion | flops 3145728 | bytes 25165824 | tf_op jit(solution)/shard_map/add | solution.py:117
  815.3 3.2 collective-permute-done.3
  818.5 2.7 select_add_fusion.1
  824.4 8.4 pad_maximum_fusion.1
  832.8 9.0 all-to-all-start.1
  841.8 72.7 %all-to-all-done.1 = bf16[4,384,1024]{2,0,1:T(4,128)(2,1)} async-done(((bf16[4,384,1024]{2,0,1:T(4,128)(2,1)}), bf16[4,384,1024]{2,0,1:T(4,128)(2,1)}, u32[]{:S(2)}, u32[]{:S(2)}) %all-to-all-start.1) | async-done | bytes 3145760 | tf_op jit(solution)/shard_map/all_to_all | solution.py:92
  914.5 3.8 gather_fusion.2
  918.4 3.0 fusion.53
  923.5 10.1 %psum.15 = f32[192]{0:T(256)S(1)} all-reduce(f32[192]{0:T(256)S(1)} %fusion.31), channel_id=1, replica_groups=mesh['seq'=64,'head'=4] {'head'}, use_global_device_ids=true, to_apply=%region_12.13 | all-reduce | flops 192 | bytes 1536 | tf_op jit(solution)/shard_map/psum | solution.py:213
  (143 shorter events, 82.5 us)
Async XLA Ops:
  0.6 400.7 %copy-start = (s32[16,96,96]{2,1,0:T(8,128)S(1)}, s32[16,96,96]{2,1,0:T(8,128)}, u32[]{:S(2)}) copy-start(s32[16,96,96]{2,1,0:T(8,128)} %param.13) | copy-start | bytes 1769476
  126.2 1.7 copy-start.2
  127.9 2.4 copy-start.7
  127.9 3.6 copy-start.6
  129.7 250.7 %collective-permute-start = (bf16[2,384,1024]{2,0,1:T(2,128)(2,1)S(1)}, bf16[2,384,1024]{2,0,1:T(2,128)(2,1)}, u32[]{:S(2)}, u32[]{:S(2)}) collective-permute-start(bf16[2,384,1024]{2,0,1:T(2,128)(2,1)S(1)} %slice.68), channel_id=1, source_target_pairs={{0,4},{4,0},{8,12},{12,8},{16,20},{20,16},{24,28},{28,24},{32,36},... | collective-permute-start | bytes 4718600 | tf_op jit(solution)/shard_map/ppermute | solution.py:17
  397.0 65.4 %collective-permute-start.1 = (bf16[2,768,1024]{2,0,1:T(2,128)(2,1)}, bf16[2,768,1024]{2,0,1:T(2,128)(2,1)}, u32[]{:S(2)}, u32[]{:S(2)}) collective-permute-start(bf16[2,768,1024]{2,0,1:T(2,128)(2,1)} %broadcast_select_fusion.2), channel_id=1, source_target_pairs={{0,8},{4,12},{8,0},{12,4},{16,24},{20,28},{24,16},{28,20},{32,40},... | collective-permute-start | bytes 9437192 | tf_op jit(solution)/shard_map/ppermute | solution.py:17
  406.4 2.3 copy-start.3
  669.5 131.6 %collective-permute-start.2 = (f32[2,768,1024]{2,0,1:T(2,128)}, f32[2,768,1024]{2,0,1:T(2,128)S(1)}, u32[]{:S(2)}, u32[]{:S(2)}) collective-permute-start(f32[2,768,1024]{2,0,1:T(2,128)} %broadcast_select_fusion.1), channel_id=1, source_target_pairs={{0,8},{4,12},{8,0},{12,4},{16,24},{20,28},{24,16},{28,20},{32,40},... | collective-permute-start | bytes 18874376 | tf_op jit(solution)/shard_map/ppermute | solution.py:17
  812.7 5.7 collective-permute-start.3
  832.8 81.8 %all-to-all-start.1 = ((bf16[4,384,1024]{2,0,1:T(4,128)(2,1)}), bf16[4,384,1024]{2,0,1:T(4,128)(2,1)}, u32[]{:S(2)}, u32[]{:S(2)}) async-start(bf16[4,384,1024]{2,0,1:T(4,128)(2,1)} %pad_maximum_fusion.1), calls=%async_computation.1 | async-start | bytes 6291456 | tf_op jit(solution)/shard_map/all_to_all | solution.py:92
  921.4 1.7 copy-start.4
  921.4 13.3 %copy-start.5 = (bf16[1,192,1024]{2,0,1:T(2,128)(2,1)S(1)}, bf16[1,192,1024]{2,0,1:T(2,128)(2,1)}, u32[]{:S(2)}) copy-start(bf16[1,192,1024]{2,0,1:T(2,128)(2,1)} %get-tuple-element.226) | copy-start | bytes 1179652
  922.3 13.3 %copy-start.1 = (s32[16,96,96]{2,1,0:T(8,128)S(1)}, s32[16,96,96]{2,1,0:T(8,128)}, u32[]{:S(2)}) copy-start(s32[16,96,96]{2,1,0:T(8,128)} %param.13) | copy-start | bytes 1769476
where the time goes:
time: 946 us; the launch traced here: 936 us
  blocking collectives  352 us (37%)
  waiting for transfers between devices  257 us (27%)
  local copies, waits for them, and re-layouts  128 us (14%)
  other arithmetic  104 us (11%)
  matrix products  70.3 us (7%)
  loops' own time  11.8 us (1%)
  starting transfers between devices  10.3 us (1%)
    unnamed x1, blocking collectives  249 us
    ppermute x4, waiting for transfers between devices, from_partner(): return lax.ppermute(value, axis, pairs)  184 us
    all_to_all x1, blocking collectives, dispatch_rows(): lax.all_to_all(outgoing, 'seq', split_axis=1, concat_axis=1, tiled=True)  83.7 us
    all_to_all x1, waiting for transfers between devices, combine_rows(): lax.all_to_all(outgoing, 'seq', split_axis=1, concat_axis=1, tiled=True)  72.7 us
    dynamic_update_slice x8, local copies, waits for them, and re-layouts, one_head(): lax.dynamic_update_slice_in_dim(side_acc, jnp.stack([key_part, value_part...  53.5 us
    select_n x2, other arithmetic, collect(): jnp.where(lower_side, jnp.concatenate([combined, partner_piece], along),...  47.3 us
    dot_general x16, matrix products, contract_last(): lax.dot_general(left_side, right_side, (((1,), (1,)), ((), ())), preferre...  29.5 us
    scatter x1, local copies, waits for them, and re-layouts, per_device(): jnp.zeros((4, received, features), jnp.bfloat16).at[:, send_slot]  22.8 us
  transfers between devices with their start and end apart: 5, of which 4 were waited for; matrix products, arithmetic and copies ran while one was open for 2% of the time, Pallas kernels for 0%

commit v1 on v0

--- a/solution.py
+++ b/solution.py
@@ -9,6 +9,12 @@
 BLK = 128
 NEG_FILL = -1e30
 EPSILON = 1e-05
+
+
+def stacked_exchange(x, axis, split, join):
+    shards = jnp.split(x, lax.axis_size(axis), axis=split)
+    incoming = lax.all_to_all(jnp.stack(shards), axis, 0, 0)
+    return jnp.concatenate(incoming, axis=join)
 
 
 def from_partner(value, axis, bit):
@@ -89,7 +95,7 @@
 
 
 def combine_rows(outgoing):
-    return lax.all_to_all(outgoing, "seq", split_axis=1, concat_axis=1, tiled=True)
+    return stacked_exchange(outgoing, "seq", 1, 1)
 
 
 def collect(local_piece, member, along, swapper):

time: 946 us -> 900 us (0.951)
  local copies, waits for them, and re-layouts: 128 us -> 81.4 us
  loops' own time: 11.8 us -> 0.49 us
  starting transfers between devices: 10.3 us -> 19.9 us
    dynamic_update_slice x8 -> x0, local copies, waits for them, and re-layouts: 53.5 us -> none  [one_head(): lax.dynamic_update_slice_in_dim(side_acc, jnp.stack([key_part, value_part...]
    another operation x1, loops' own time: 11.8 us -> 0.49 us  [forward_heads(): lax.fori_loop(0, head_count, one_head, (attended, query_grad, side_result))]
    dynamic_update_slice x0 -> x8, other arithmetic: none -> 10.9 us  [one_head(): lax.dynamic_update_slice_in_dim(side_acc, jnp.stack([key_part, value_part...]
where the time goes in v1:
time: 900 us; the launch traced here: 890 us
  blocking collectives  352 us (39%)
  waiting for transfers between devices  260 us (29%)
  other arithmetic  103 us (11%)
  local copies, waits for them, and re-layouts  81.4 us (9%)
  matrix products  70.3 us (8%)
  starting transfers between devices  19.9 us (2%)
    unnamed x1, blocking collectives  249 us
    ppermute x4, waiting for transfers between devices, from_partner(): return lax.ppermute(value, axis, pairs)  187 us
    all_to_all x1, blocking collectives, dispatch_rows(): lax.all_to_all(outgoing, 'seq', split_axis=1, concat_axis=1, tiled=True)  83.8 us
    all_to_all x1, waiting for transfers between devices, stacked_exchange(): incoming = lax.all_to_all(jnp.stack(shards), axis, 0, 0)  72.7 us
    select_n x2, other arithmetic, collect(): jnp.where(lower_side, jnp.concatenate([combined, partner_piece], along),...  47.3 us
    dot_general x16, matrix products, contract_last(): lax.dot_general(left_side, right_side, (((1,), (1,)), ((), ())), preferre...  29.5 us
    scatter x1, local copies, waits for them, and re-layouts, per_device(): jnp.zeros((4, received, features), jnp.bfloat16).at[:, send_slot]  22.8 us
  transfers between devices with their start and end apart: 5, of which 4 were waited for; matrix products, arithmetic and copies ran while one was open for 2% of the time, Pallas kernels for 0%

profile of v1, /device:TPU:2, one launch (start us, length us, event | category | flops | bytes accessed | tf_op | source)
XLA Modules:
  0.0 889.5 jit_solution(11847647258435794512)
XLA Ops:
  3.5 10.0 %psum.14 = f32[192]{0:T(256)S(1)} all-reduce(f32[192]{0:T(256)S(1)} %fusion.30), channel_id=1, replica_groups=mesh['seq'=64,'head'=4] {'head'}, use_global_device_ids=true, to_apply=%region_2.3 | all-reduce | flops 192 | bytes 1536 | tf_op jit(solution)/shard_map/psum | solution.py:180
  17.2 2.5 broadcast_in_dim.72
  19.7 22.8 %scatter_fusion = bf16[4,384,1024]{2,0,1:T(4,128)(2,1)} fusion(bf16[4,384,1024]{2,0,1:T(4,128)(2,1)} %broadcast_in_dim.72, s32[192]{0:T(256)S(1)} %bitcast.351, bf16[192,4,1024]{2,1,0:T(4,128)(2,1)S(1)} %copy.50), kind=kCustom, calls=%fused_computation.3 | custom fusion | bytes 4719360 | tf_op jit(solution)/shard_map/scatter | solution.py:198
  42.5 83.8 %all_to_all.10 = bf16[4,384,1024]{2,0,1:T(4,128)(2,1)S(1)} all-to-all(bf16[4,384,1024]{2,0,1:T(4,128)(2,1)} %scatter_fusion), channel_id=1, replica_groups=mesh['seq'=64,'head'=4] {'seq'}, dimensions={1} | all-to-all | bytes 6291456 | tf_op jit(solution)/shard_map/all_to_all | solution.py:94
  126.4 1.7 copy-done.3
  128.0 1.8 slice.68
  132.0 248.5 %all-reduce = s32[12288]{0:T(1024)S(1)} all-reduce(s32[12288]{0:T(1024)S(1)} %dynamic-update-slice), channel_id=2, replica_groups=mesh['seq'=64,'head'=4] {'seq'}, use_global_device_ids=true, to_apply=%add | all-reduce | flops 12288 | bytes 98304
  380.5 16.6 %broadcast_select_fusion.1 = bf16[2,768,1024]{2,0,1:T(2,128)(2,1)} fusion(pred[]{:T(512)S(6)} %eq.66, bf16[2,384,1024]{2,0,1:T(2,128)(2,1)} %collective-permute-done, bf16[2,384,1024]{2,0,1:T(2,128)(2,1)S(1)} %slice.68), kind=kLoop, calls=%fused_computation.39 | loop fusion | flops 4718592 | bytes 6291457 | tf_op jit(solution)/shard_map/jit(_where)/select_n | solution.py:106
  397.1 9.6 %collective-permute-start.1 = (bf16[2,768,1024]{2,0,1:T(2,128)(2,1)}, bf16[2,768,1024]{2,0,1:T(2,128)(2,1)}, u32[]{:S(2)}, u32[]{:S(2)}) collective-permute-start(bf16[2,768,1024]{2,0,1:T(2,128)(2,1)} %broadcast_select_fusion.1), channel_id=1, source_target_pairs={{0,8},{4,12},{8,0},{12,4},{16,24},{20,28},{24,16},{28,20},{32,40},... | collective-permute-start | bytes 9437192 | tf_op jit(solution)/shard_map/ppermute | solution.py:23
  412.1 3.7 gather_fusion.1
  415.9 1.5 fusion.26
  418.2 2.2 fusion.52
  421.9 49.9 %collective-permute-done.1 = bf16[2,768,1024]{2,0,1:T(2,128)(2,1)} collective-permute-done((bf16[2,768,1024]{2,0,1:T(2,128)(2,1)}, bf16[2,768,1024]{2,0,1:T(2,128)(2,1)}, u32[]{:S(2)}, u32[]{:S(2)}) %collective-permute-start.1) | collective-permute-done | bytes 3145760 | tf_op jit(solution)/shard_map/ppermute | solution.py:23
  471.8 30.7 %broadcast_select_fusion = bf16[2,1536,1024]{2,0,1:T(2,128)(2,1)S(1)} fusion(pred[]{:T(512)S(6)} %eq.65, bf16[2,768,1024]{2,0,1:T(2,128)(2,1)} %collective-permute-done.1, bf16[2,768,1024]{2,0,1:T(2,128)(2,1)} %broadcast_select_fusion.1), kind=kLoop, calls=%fused_computation.37 | loop fusion | flops 9437184 | bytes 12582913 | tf_op jit(solution)/shard_map/jit(_where)/select_n | solution.py:106
  502.6 9.8 %fusion.51 = (bf16[1,1536,1024]{2,0,1:T(2,128)(2,1)S(1)}, bf16[1,1536,1024]{2,0,1:T(2,128)(2,1)}) fusion(bf16[2,1536,1024]{2,0,1:T(2,128)(2,1)S(1)} %broadcast_select_fusion), kind=kLoop, calls=%fused_computation.264 | loop fusion | bytes 12582912 | tf_op jit(solution)/shard_map/slice | solution.py:208
  512.4 8.0 copy_bitcast_fusion
  520.6 6.2 broadcast_in_dim.71
  526.8 88.3 %while.17 = (s32[]{:T(128)}, bf16[384,1024]{1,0:T(8,128)(2,1)S(1)}, bf16[384,1024]{1,0:T(8,128)(2,1)S(1)}, f32[2,1536,1024]{2,1,0:T(8,128)}, bf16[384,1024]{1,0:...) while((s32[]{:T(128)}, bf16[384,1024]{1,0:T(8,128)(2,1)S(1)}, ...), condition=%wide.region_10.11_spmd, body=%wide.region_6.10_spmd.sunk | while | flops 915946752 | bytes 33441472 | solution.py:166
  527.0 1.7 fusion.77
  529.3 2.0 multiply_reduce_fusion.2
  538.0 1.7 fusion.77
  540.3 2.0 multiply_reduce_fusion.2
  549.0 1.7 fusion.77
  551.4 2.0 multiply_reduce_fusion.2
  555.2 1.5 fusion.80
  560.0 1.7 fusion.77
  562.4 2.0 multiply_reduce_fusion.2
  571.0 1.7 fusion.77
  573.4 2.0 multiply_reduce_fusion.2
  577.2 1.5 fusion.80
  582.1 1.7 fusion.77
  584.4 2.0 multiply_reduce_fusion.2
  593.1 1.7 fusion.77
  595.4 2.0 multiply_reduce_fusion.2
  599.2 1.5 fusion.80
  604.0 1.7 fusion.77
  606.4 2.0 multiply_reduce_fusion.2
  615.0 6.1 slice_select_fusion
  621.5 131.2 %collective-permute-done.2 = f32[2,768,1024]{2,1,0:T(8,128)} collective-permute-done((f32[2,768,1024]{2,1,0:T(8,128)S(1)}, f32[2,768,1024]{2,1,0:T(8,128)}, u32[]{:S(2)}, u32[]{:S(2)}) %collective-permute-start.2) | collective-permute-done | bytes 6291488 | tf_op jit(solution)/shard_map/ppermute | solution.py:23
  752.7 12.0 %select_add_fusion = f32[2,768,1024]{2,1,0:T(8,128)} fusion(f32[2,768,1024]{2,1,0:T(8,128)} %collective-permute-done.2, f32[2,1536,1024]{2,1,0:T(8,128)} %get-tuple-element.162, pred[]{:T(512)S(6)} %eq.65), kind=kLoop, calls=%fused_computation.38 | loop fusion | flops 3145728 | bytes 25165824 | tf_op jit(solution)/shard_map/add | solution.py:123
  764.7 3.7 slice_select_fusion.1
  768.5 5.6 collective-permute-done.3
  778.4 7.9 copy.60
  786.3 9.2 %all-to-all-start.1 = ((bf16[64,4,6,1024]{3,1,2,0:T(4,128)(2,1)}), bf16[64,4,6,1024]{3,1,2,0:T(4,128)(2,1)}, u32[]{:S(2)}, u32[]{:S(2)}) async-start(bf16[64,4,6,1024]{3,1,2,0:T(4,128)(2,1)} %copy.60), calls=%async_computation.1 | async-start | bytes 6291456 | tf_op jit(solution)/shard_map/all_to_all | solution.py:16
  795.6 72.7 %all-to-all-done.1 = bf16[64,4,6,1024]{3,1,2,0:T(4,128)(2,1)} async-done(((bf16[64,4,6,1024]{3,1,2,0:T(4,128)(2,1)}), bf16[64,4,6,1024]{3,1,2,0:T(4,128)(2,1)}, u32[]{:S(2)}, u32[]{:S(2)}) %all-to-all-start.1) | async-done | bytes 3145760 | tf_op jit(solution)/shard_map/all_to_all | solution.py:16
  868.3 3.8 gather_fusion.2
  872.2 3.0 fusion.53
  877.2 10.1 %psum.15 = f32[192]{0:T(256)S(1)} all-reduce(f32[192]{0:T(256)S(1)} %fusion.31), channel_id=1, replica_groups=mesh['seq'=64,'head'=4] {'head'}, use_global_device_ids=true, to_apply=%region_12.13 | all-reduce | flops 192 | bytes 1536 | tf_op jit(solution)/shard_map/psum | solution.py:219
  (200 shorter events, 77.7 us)
Async XLA Ops:
  0.6 410.1 %copy-start = (s32[16,96,96]{2,1,0:T(8,128)S(1)}, s32[16,96,96]{2,1,0:T(8,128)}, u32[]{:S(2)}) copy-start(s32[16,96,96]{2,1,0:T(8,128)} %param.13) | copy-start | bytes 1769476
  42.5 87.9 %copy-start.8 = (u32[256]{0:T(256)S(1)}, u32[256]{0:T(256)}, u32[]{:S(2)}) copy-start(u32[256]{0:T(256)} %constant.244) | copy-start | bytes 3076
  42.5 89.1 %copy-start.7 = (s32[192,1]{0,1:T(1,128)S(1)}, s32[192,1]{0,1:T(1,128)}, u32[]{:S(2)}) copy-start(s32[192,1]{0,1:T(1,128)} %param.12) | copy-start | bytes 2308
  126.4 1.7 copy-start.3
  129.8 250.7 %collective-permute-start = (bf16[2,384,1024]{2,0,1:T(2,128)(2,1)S(1)}, bf16[2,384,1024]{2,0,1:T(2,128)(2,1)}, u32[]{:S(2)}, u32[]{:S(2)}) collective-permute-start(bf16[2,384,1024]{2,0,1:T(2,128)(2,1)S(1)} %slice.68), channel_id=1, source_target_pairs={{0,4},{4,0},{8,12},{12,8},{16,20},{20,16},{24,28},{28,24},{32,36},... | collective-permute-start | bytes 4718600 | tf_op jit(solution)/shard_map/ppermute | solution.py:23
  397.1 74.7 %collective-permute-start.1 = (bf16[2,768,1024]{2,0,1:T(2,128)(2,1)}, bf16[2,768,1024]{2,0,1:T(2,128)(2,1)}, u32[]{:S(2)}, u32[]{:S(2)}) collective-permute-start(bf16[2,768,1024]{2,0,1:T(2,128)(2,1)} %broadcast_select_fusion.1), channel_id=1, source_target_pairs={{0,8},{4,12},{8,0},{12,4},{16,24},{20,28},{24,16},{28,20},{32,40},... | collective-permute-start | bytes 9437192 | tf_op jit(solution)/shard_map/ppermute | solution.py:23
  415.8 2.3 copy-start.4
  621.1 131.6 %collective-permute-start.2 = (f32[2,768,1024]{2,1,0:T(8,128)S(1)}, f32[2,768,1024]{2,1,0:T(8,128)}, u32[]{:S(2)}, u32[]{:S(2)}) collective-permute-start(f32[2,768,1024]{2,1,0:T(8,128)S(1)} %slice_select_fusion), channel_id=1, source_target_pairs={{0,8},{4,12},{8,0},{12,4},{16,24},{20,28},{24,16},{28,20},{32,40},... | collective-permute-start | bytes 18874376 | tf_op jit(solution)/shard_map/ppermute | solution.py:23
  764.7 9.4 %copy-start.2 = (f32[2,768,1024]{2,1,0:T(8,128)S(1)}, f32[2,768,1024]{2,1,0:T(8,128)}, u32[]{:S(2)}) copy-start(f32[2,768,1024]{2,1,0:T(8,128)} %select_add_fusion) | copy-start | bytes 18874372
  768.4 5.7 collective-permute-start.3
  786.3 82.0 %all-to-all-start.1 = ((bf16[64,4,6,1024]{3,1,2,0:T(4,128)(2,1)}), bf16[64,4,6,1024]{3,1,2,0:T(4,128)(2,1)}, u32[]{:S(2)}, u32[]{:S(2)}) async-start(bf16[64,4,6,1024]{3,1,2,0:T(4,128)(2,1)} %copy.60), calls=%async_computation.1 | async-start | bytes 6291456 | tf_op jit(solution)/shard_map/all_to_all | solution.py:16
  872.1 4.8 copy-start.5
  872.1 17.2 %copy-start.1 = (s32[16,96,96]{2,1,0:T(8,128)S(1)}, s32[16,96,96]{2,1,0:T(8,128)}, u32[]{:S(2)}) copy-start(s32[16,96,96]{2,1,0:T(8,128)} %param.13) | copy-start | bytes 1769476
  875.2 13.3 %copy-start.6 = (bf16[1,192,1024]{2,0,1:T(2,128)(2,1)S(1)}, bf16[1,192,1024]{2,0,1:T(2,128)(2,1)}, u32[]{:S(2)}) copy-start(bf16[1,192,1024]{2,0,1:T(2,128)(2,1)} %get-tuple-element.244) | copy-start | bytes 1179652
